TPU v7x, 32 devices: a whole 2x2x4 slice. The times are simulated.
32 devices in a mesh: replica: 2 (over core), shard: 16 (over z, y, x).
Axes of the slice: x: 2, y: 2, z: 4, core: 2. Of those that a mesh axis runs over, the one named last changes fastest.
Arguments:
- dense_input: bfloat16 [4096, 256], P(('replica', 'shard')), may hold values from -6 to 6
- bag_rows: int32 [4096, 2, 16], P(('replica', 'shard')), may hold values from 0 to 8191, as said below
- bag_lengths: int32 [4096, 2], P(('replica', 'shard')), may hold values from 1 to 16
- bag_weights: bfloat16 [4096, 2, 16], P(('replica', 'shard')), may hold values from 0.5 to 2
- labels: int32 [4096], P(('replica', 'shard')), may hold values 0 or 1
- embedding: float32 [8192, 2, 256], P('shard'), may hold values from -2 to 2
- first_moment: float32 [8192, 2, 256], P('shard'), may hold values from -6 to 6
- second_moment: float32 [8192, 2], P('shard'), may hold values from 0.5 to 8
- cross_weight: bfloat16 [768, 768], replicated, may hold values from -0.21875 to 0.21875
- hidden_weight: bfloat16 [768, 4096], replicated, may hold values from -0.21875 to 0.21875
- head_weight: bfloat16 [4096], replicated, may hold values from -0.09375 to 0.09375
Outputs:
- new_first: float32 [8192, 2, 256], P('shard')
- new_second: float32 [8192, 2], P('shard')
- row_step: float32 [8192, 2, 256], P('shard')
Inputs may be any that keep to these rules, and one draw needn't show every extreme that they name: `bag_rows`: call the rows k * 512 to (k + 1) * 512 - 1 those of owner k. For each table, all slots of one device's 128 samples (used or not) name at most 32 distinct rows of any one owner, and every device names exactly 32 distinct rows of some owner in each table. Row indices may be held and sent in any lossless form.
All inputs are finite; a program needn't handle non-finite values. No bound on the sum of `labels` on one device may be relied on, other than what follows from the above.
Results may differ from a plain program's by a relative error of at most 0.0038.
The roundings to bfloat16 on the way count: a program that leaves them out, or rounds other values in their place, can miss the bound.
Values may be sent and summed in bfloat16 or wider, within the bound.
A program may use at most 128 MiB of HBM per device.

v0:
```python
import functools

import jax
import jax.numpy as jnp
from jax import lax
from jax.experimental import pallas as pl
from jax.experimental.pallas import tpu as pltpu
from jax.sharding import PartitionSpec as P

loss_scale = 64.0
beta_first = 0.9
beta_second = 0.99
epsilon = 1e-08
CAP = 32
F32 = jnp.float32
BF16 = jnp.bfloat16
MESH = pl.DeviceIdType.MESH


def dot(a, b, ca, cb):
    return lax.dot_general(a, b, (((ca,), (cb,)), ((), ())), preferred_element_type=F32)


def vmem(count):
    return [pl.BlockSpec(memory_space=pltpu.VMEM)] * count


def column(row, eye):
    size = eye.shape[0]
    return jnp.concatenate(
        [
            jnp.sum(jnp.where(eye, row[:, lo : lo + size], 0.0), axis=1, keepdims=True)
            for lo in range(0, row.shape[1], size)
        ],
        axis=0,
    )


def flat(col, eye):
    size = eye.shape[0]
    return jnp.concatenate(
        [
            jnp.sum(jnp.where(eye, col[lo : lo + size], 0.0), axis=0, keepdims=True)
            for lo in range(0, col.shape[0], size)
        ],
        axis=1,
    )


def diagonal(size):
    a = lax.broadcasted_iota(jnp.int32, (size, size), 0)
    return a == lax.broadcasted_iota(jnp.int32, (size, size), 1)


def rank_rows(n, own_rows, ids, lengths, upper, loc_ref):
    slots, samples = ids.shape
    shift = own_rows.bit_length() - 1
    own_iota = lax.broadcasted_iota(jnp.int32, (n, samples), 0)
    loc_iota = lax.broadcasted_iota(jnp.int32, (own_rows, samples), 0)
    usable = lax.broadcasted_iota(jnp.int32, (slots, samples), 0) < lengths
    own = lax.shift_right_logical(ids, shift)
    loc = ids & (own_rows - 1)
    own_used = jnp.where(usable, own, -1)
    masks = [own_iota == own_used[s : s + 1] for s in range(slots)]
    all_own = jnp.concatenate([jnp.where(m, 1.0, 0.0).astype(BF16) for m in masks], axis=1)
    all_loc = jnp.concatenate(
        [jnp.where(loc_iota == loc[s : s + 1], 1.0, 0.0).astype(BF16) for s in range(slots)],
        axis=1,
    )
    seen = dot(all_own, all_loc, 1, 1) > 0.0
    rank = dot(jnp.where(seen, 1.0, 0.0).astype(BF16), upper, 1, 0)
    loc_ref[...] = all_loc
    return jnp.where(seen, rank, -1.0)


def coefficients(n, own_rows, ids, lengths, weights, q, loc_ref, ct_ref):
    slots, samples = ids.shape
    shift = own_rows.bit_length() - 1
    own_iota = lax.broadcasted_iota(jnp.int32, (n, samples), 0)
    usable = lax.broadcasted_iota(jnp.int32, (slots, samples), 0) < lengths
    own = lax.shift_right_logical(ids, shift)
    mass = jnp.where(usable, weights.astype(F32), 0.0)
    here = dot(q.astype(BF16), loc_ref[...], 1, 0)
    places = []
    for s in range(slots):
        mine = jnp.where(own_iota == own[s : s + 1], here[:, s * samples : (s + 1) * samples], 0.0)
        place = jnp.sum(mine, axis=0, keepdims=True)
        places.append(own[s : s + 1] * CAP + place.astype(jnp.int32))
    step = 128
    for base in range(0, n * CAP, step):
        pos_iota = lax.broadcasted_iota(jnp.int32, (step, samples), 0) + base
        total = jnp.zeros((step, samples), F32)
        for s in range(slots):
            total = total + jnp.where(pos_iota == places[s], mass[s : s + 1], 0.0)
        ct_ref[base : base + step, :] = total.astype(BF16)


def selector(rows):
    want = lax.broadcasted_iota(jnp.int32, (CAP, rows[0].shape[1]), 0).astype(F32)
    return jnp.concatenate(
        [jnp.where(want == row, 1.0, 0.0).astype(BF16) for row in rows], axis=0
    )


def update_kernel(
    n, reps,
    rows_ref, len_ref, w_ref, dense_ref, mark_ref, head_ref, emb_hbm, cross_hbm, hidden_hbm,
    qi_ref, qo_ref, ga_ref,
    emb, cross, hid, q_out, f_out, f_in, ct, before, g_out, locs,
    load_sem, own_sem, qs, qr, rs, rr, gs, gr, xs, xr, fs, fr,
):
    me = lax.axis_index("shard")
    rep = lax.axis_index("replica")
    tables, slots, samples = rows_ref.shape
    own_rows, _, width = emb.shape
    barrier = pltpu.get_barrier_semaphore()

    def hail(d, carry):
        pl.semaphore_signal(
            barrier, inc=1, device_id=(rep, lax.rem(me + d, n)), device_id_type=MESH
        )
        return carry

    lax.fori_loop(1, n, hail, 0)
    for r in range(1, reps):
        pl.semaphore_signal(
            barrier, inc=1, device_id=(lax.rem(rep + r, reps), me), device_id_type=MESH
        )
    load_emb = pltpu.make_async_copy(emb_hbm, emb, load_sem.at[0])
    load_cross = pltpu.make_async_copy(cross_hbm, cross, load_sem.at[1])
    load_hid = pltpu.make_async_copy(hidden_hbm, hid, load_sem.at[2])
    load_emb.start()
    load_cross.start()
    load_hid.start()

    def exchange(src, dst, send, recv, t, d):
        to = lax.rem(me + d, n)
        return pltpu.make_async_remote_copy(
            src_ref=src.at[t, to],
            dst_ref=dst.at[t, me],
            send_sem=send.at[t, d],
            recv_sem=recv.at[t, d],
            device_id=(rep, to),
            device_id_type=MESH,
        )

    def each(body):
        def run(d, carry):
            body(d)
            return carry

        lax.fori_loop(1, n, run, 0)

    def keep(src, dst, t):
        copy = pltpu.make_async_copy(src.at[t, me], dst.at[t, me], own_sem)
        copy.start()
        copy.wait()

    q_send = functools.partial(exchange, q_out, qi_ref, qs, qr)
    f_send = functools.partial(exchange, f_out, f_in, rs, rr)
    g_send = functools.partial(exchange, g_out, ga_ref.at[0], gs, gr)

    r0 = lax.broadcasted_iota(jnp.int32, (own_rows, own_rows), 0)
    r1 = lax.broadcasted_iota(jnp.int32, (own_rows, own_rows), 1)
    upper = jnp.where(r0 < r1, 1.0, 0.0).astype(BF16)
    ranks = []
    for t in range(tables):
        q = rank_rows(n, own_rows, rows_ref[t], len_ref[t], upper, locs.at[t])
        q_out[t, :, 0, :] = q
        ranks.append(q)
        if t == 0:
            pl.semaphore_wait(barrier, n - 1 + reps - 1)
        each(lambda d: q_send(t, d).start())
        keep(q_out, qi_ref, t)

    load_emb.wait()
    for t in range(tables):
        low = emb[:, t, :].astype(BF16)
        each(lambda d: q_send(t, d).wait_recv())
        got = dot(selector([qi_ref[t, s] for s in range(n)]), low, 1, 0).astype(BF16)
        f_out[t] = got.reshape(n, CAP, width)
        each(lambda d: f_send(t, d).start())
        keep(f_out, f_in, t)

    def q_pass(r):
        return pltpu.make_async_remote_copy(
            src_ref=qi_ref,
            dst_ref=qo_ref.at[r - 1],
            send_sem=xs.at[r - 1],
            recv_sem=xr.at[r - 1],
            device_id=(lax.rem(rep + r, reps), me),
            device_id_type=MESH,
        )

    for r in range(1, reps):
        q_pass(r).start()

    for t in range(tables):
        coefficients(
            n, own_rows, rows_ref[t], len_ref[t], w_ref[t], ranks[t], locs.at[t], ct.at[t]
        )
    marks = column(mark_ref[...].astype(F32), diagonal(samples))
    heads = head_ref[...].astype(F32)
    lanes = heads.shape[1]

    def head_chunk(base, count):
        first = base // lanes
        return jnp.concatenate(
            [heads[first + i : first + i + 1] for i in range(count // lanes)], axis=1
        )

    part = dense_ref.shape[1]
    pieces = [dense_ref[...]]
    load_cross.wait()
    crossed = dot(pieces[0], cross[:part, :], 1, 0)
    for t in range(tables):
        each(lambda d: f_send(t, d).wait_recv())
        pieces.append(dot(ct[t], f_in[t].reshape(n * CAP, width), 0, 0).astype(BF16))
        lo = part + t * width
        crossed = crossed + dot(pieces[-1], cross[lo : lo + width, :], 1, 0)
    joined = jnp.concatenate(pieces, axis=1)
    widened = joined.astype(F32)
    layered = (widened * crossed + widened).astype(BF16)
    load_hid.wait()
    units = hid.shape[1]
    chunk = 512
    logits = jnp.zeros((samples, 1), F32)
    for base in range(0, units, chunk):
        now = dot(layered, hid[:, base : base + chunk], 1, 0)
        before[:, base : base + chunk] = now
        hidden = jnp.maximum(now, 0.0).astype(BF16).astype(F32)
        head = head_chunk(base, chunk)
        logits = logits + jnp.sum(hidden * head, axis=1, keepdims=True)
    slope = (1.0 / (1.0 + jnp.exp(-logits)) - marks) * loss_scale
    back = jnp.zeros((samples, joined.shape[1]), F32)
    for base in range(0, units, chunk):
        head = head_chunk(base, chunk)
        push = jnp.where(before[:, base : base + chunk] > 0.0, slope * head, 0.0).astype(BF16)
        back = back + dot(push, hid[:, base : base + chunk], 1, 1)
    mixed = (back * widened).astype(BF16)
    for t in range(tables):
        lo = part + t * width
        grads = back[:, lo : lo + width] * (crossed[:, lo : lo + width] + 1.0) + dot(
            mixed, cross[lo : lo + width, :], 1, 1
        )
        sums = dot(ct[t], grads.astype(BF16), 1, 0).astype(BF16)
        g_out[t] = sums.reshape(n, CAP, width)
        each(lambda d: g_send(t, d).start())
        keep(g_out, ga_ref.at[0], t)

    def pass_on(r, t, d):
        frm = lax.rem(me + n - d, n)
        return pltpu.make_async_remote_copy(
            src_ref=ga_ref.at[0, t, frm],
            dst_ref=ga_ref.at[r, t, frm],
            send_sem=fs.at[r - 1, t, d],
            recv_sem=fr.at[r - 1, t, d],
            device_id=(lax.rem(rep + r, reps), me),
            device_id_type=MESH,
        )

    for t in range(tables):
        for r in range(1, reps):
            pass_on(r, t, 0).start()

        def relay(d):
            g_send(t, d).wait_recv()
            for r in range(1, reps):
                pass_on(r, t, d).start()

        each(relay)
    for r in range(1, reps):
        q_pass(r).wait()
    for t in range(tables):
        for r in range(1, reps):
            pass_on(r, t, 0).wait()

        def finish(d):
            q_send(t, d).wait_send()
            f_send(t, d).wait_send()
            g_send(t, d).wait_send()
            for r in range(1, reps):
                pass_on(r, t, d).wait()

        each(finish)


def update(n, reps, rows, lengths, weights, dense, marks, head, embedding, cross, hidden):
    tables, slots, samples = rows.shape
    own_rows, _, width = embedding.shape
    dma = pltpu.SemaphoreType.DMA
    blocks = (tables, n, CAP, width)
    pair = dma((tables, n))
    wide = dma((reps - 1, tables, n))
    return pl.pallas_call(
        functools.partial(update_kernel, n, reps),
        out_shape=(
            jax.ShapeDtypeStruct((tables, n, 1, own_rows), F32),
            jax.ShapeDtypeStruct((reps - 1, tables, n, 1, own_rows), F32),
            jax.ShapeDtypeStruct((reps,) + blocks, BF16),
        ),
        in_specs=vmem(6) + [pl.BlockSpec(memory_space=pl.ANY)] * 3,
        out_specs=tuple(vmem(3)),
        scratch_shapes=[
            pltpu.VMEM(embedding.shape, F32),
            pltpu.VMEM(cross.shape, BF16),
            pltpu.VMEM(hidden.shape, BF16),
            pltpu.VMEM((tables, n, 1, own_rows), F32),
            pltpu.VMEM(blocks, BF16),
            pltpu.VMEM(blocks, BF16),
            pltpu.VMEM((tables, n * CAP, samples), BF16),
            pltpu.VMEM((samples, hidden.shape[1]), F32),
            pltpu.VMEM(blocks, BF16),
            pltpu.VMEM((tables, own_rows, slots * samples), BF16),
            dma((3,)),
            dma,
            pair, pair, pair, pair, pair, pair,
            dma((reps - 1,)), dma((reps - 1,)),
            wide, wide,
        ],
        compiler_params=pltpu.CompilerParams(collective_id=0, has_side_effects=True),
        name="update",
    )(rows, lengths, weights, dense, marks, head, embedding, cross, hidden)


def adam_kernel(reps, ga_ref, q_ref, qo_ref, m_ref, v_ref, nm_ref, nv_ref, st_ref):
    tables, n, _, blk = q_ref.shape
    width = m_ref.shape[2]
    eye = diagonal(128)
    for t in range(tables):
        m = m_ref[:, t, :]
        v = column(v_ref[t : t + 1, :], eye)
        first = second = step = None
        for r in range(reps):
            src = q_ref if r == 0 else qo_ref.at[r - 1]
            rows = [src[t, s] for s in range(n)]
            named = rows[0]
            for row in rows[1:]:
                named = jnp.maximum(named, row)
            touched = column(named, eye) >= 0.0
            grad = dot(selector(rows), ga_ref[r, t].reshape(n * CAP, width), 0, 0)
            new_m = jnp.where(touched, beta_first * m + (1.0 - beta_first) * grad, m)
            mean = jnp.mean(grad * grad, axis=1, keepdims=True)
            new_v = jnp.where(touched, beta_second * v + (1.0 - beta_second) * mean, v)
            scale = jnp.where(touched, 1.0 / (jnp.sqrt(new_v) + epsilon), 0.0)
            new_s = new_m * scale
            first = new_m if r == 0 else first + new_m
            second = new_v if r == 0 else second + new_v
            step = new_s if r == 0 else step + new_s
        nm_ref[:, t, :] = first * (1.0 / reps)
        nv_ref[t : t + 1, :] = flat(second, eye) * (1.0 / reps)
        st_ref[:, t, :] = step * (1.0 / reps)


def adam(ga, q, qo, first_moment, second_moment, reps):
    tables, n, _, own_rows = q.shape
    width = first_moment.shape[2]
    blk = own_rows // 2
    mom = pl.BlockSpec((blk, tables, width), lambda i: (i, 0, 0))
    sec = pl.BlockSpec((tables, blk), lambda i: (0, i))
    return pl.pallas_call(
        functools.partial(adam_kernel, reps),
        out_shape=(
            jax.ShapeDtypeStruct(first_moment.shape, F32),
            jax.ShapeDtypeStruct(second_moment.shape, F32),
            jax.ShapeDtypeStruct(first_moment.shape, F32),
        ),
        grid=(own_rows // blk,),
        in_specs=[
            pl.BlockSpec(ga.shape, lambda i: (0,) * 5, pipeline_mode=pl.Buffered(1)),
            pl.BlockSpec((tables, n, 1, blk), lambda i: (0, 0, 0, i)),
            pl.BlockSpec((reps - 1, tables, n, 1, blk), lambda i: (0, 0, 0, 0, i)),
            mom,
            sec,
        ],
        out_specs=(mom, sec, mom),
        name="adam",
    )(ga, q, qo, first_moment, second_moment)


def local(
    reps,
    n,
    dense_input,
    bag_rows,
    bag_lengths,
    bag_weights,
    labels,
    embedding,
    first_moment,
    second_moment,
    cross_weight,
    hidden_weight,
    head_weight,
):
    q, q_other, ga = update(
        n,
        reps,
        jnp.transpose(bag_rows, (1, 2, 0)),
        jnp.transpose(bag_lengths)[:, None, :],
        jnp.transpose(bag_weights, (1, 2, 0)),
        dense_input,
        labels[None, :],
        head_weight.reshape(-1, 128),
        embedding,
        cross_weight,
        hidden_weight,
    )
    first, second, step = adam(
        ga, q, q_other, first_moment, jnp.transpose(second_moment), reps
    )
    return first, jnp.transpose(second), step


def solution(mesh):
    placed = (
        P(("replica", "shard"), None),
        P(("replica", "shard"), None, None),
        P(("replica", "shard"), None),
        P(("replica", "shard"), None, None),
        P(("replica", "shard")),
        P("shard", None, None),
        P("shard", None, None),
        P("shard", None),
        P(),
        P(),
        P(),
    )
    return jax.shard_map(
        functools.partial(local, mesh.shape["replica"], mesh.shape["shard"]),
        mesh=mesh,
        in_specs=placed,
        out_specs=(P("shard", None, None), P("shard", None), P("shard", None, None)),
        check_vma=False,
    )
```

profile of v0, /device:TPU:1, one launch (start us, length us, event | category | flops | bytes accessed | tf_op | source)
XLA Modules:
  0.0 50.7 jit_solution(12334748508128066880)
XLA Ops:
  0.6 44.1 %update.1 = (f32[2,16,1,512]{3,2,1,0:T(1,128)}, f32[1,2,16,1,512]{4,3,2,1,0:T(1,128)}, bf16[2,2,16,32,256]{4,3,2,1,0:T(8,128)(2,1)}) custom-call(s32[2,16,128]{2,1,0:T(8,128)} %bitcast.9, s32[2,1,128]{2,1,0:T(1,128)} %bitcast.13, bf16[2,16,128]{2,1,0:T(8,128)(2,1)} %bitcast.10, bf16[128,256]{1,0:T(8,128)(2,1)} %dense_ref.1, s32[1,128]{1,0:T(1,128)} %bitcast.14, ...), custom_call_target="tpu_custom_call" | custom-call | tf_op jit(solution)/shard_map/update/pallas_call | solution.py:295
  44.7 6.0 %adam.1 = (f32[512,2,256]{2,1,0:T(2,128)}, f32[2,512]{1,0:T(2,128)}, f32[512,2,256]{2,1,0:T(2,128)}) custom-call(bf16[2,2,16,32,256]{4,3,2,1,0:T(8,128)(2,1)} %get-tuple-element.9.ga_ref, f32[2,16,1,512]{3,2,1,0:T(1,128)} %get-tuple-element.10.q_ref, f32[1,2,16,1,512]{4,3,2,1,0:T(1,128)} %get-tuple-element.11.qo_ref, f32[512,2,256]{2,1,0:T(2,128)} %m_ref.1, ...), custom_call_target="tpu_custom_call" | custom-call | tf_op jit(solution)/shard_map/adam/pallas_call | solution.py:361
where the time goes:
time: 51 us; the launch traced here: 50.7 us
  Pallas kernels  50.1 us (98%)
  between operations  0.64 us (1%)
    pallas_call x1, Pallas kernels, update(): pl.pallas_call(functools.partial(update_kernel, n, reps), out_shape=(jax....  44.1 us
    pallas_call x1, Pallas kernels, adam(): pl.pallas_call(functools.partial(adam_kernel, reps), out_shape=(jax.Shape...  6 us

commit v1 on v0

--- a/solution.py
+++ b/solution.py
@@ -102,12 +102,50 @@
     )
 
 
+def place_rows(q_ref, sel_ref, hit_ref):
+    n, _, own_rows = q_ref.shape
+    q = jnp.concatenate([q_ref[s] for s in range(n)], axis=0).astype(BF16)
+    source = lax.broadcasted_iota(jnp.int32, (n, n * CAP), 1) // CAP
+    spread = jnp.where(lax.broadcasted_iota(jnp.int32, (n, n * CAP), 0) == source, 1.0, 0.0)
+    ranks = dot(q, spread.astype(BF16), 0, 0)
+    want = (lax.broadcasted_iota(jnp.int32, ranks.shape, 1) & (CAP - 1)).astype(F32)
+    sel_ref[...] = jnp.where(ranks == want, 1.0, 0.0).astype(BF16)
+    hit_ref[...] = jnp.max(ranks, axis=1, keepdims=True)
+
+
+def adam_rows(reps, t, acc, hit, mom, v_ref, nm_ref, nv_ref, st_ref):
+    own_rows = v_ref.shape[1]
+    step = 128
+    eye = diagonal(step)
+    for lo in range(0, own_rows, step):
+        at = slice(lo, lo + step)
+        m = mom[at, t, :]
+        v = column(v_ref[t : t + 1, at], eye)
+        first = second = move = None
+        for r in range(reps):
+            grad = acc[r, at, :]
+            touched = hit[t, r, at, :] >= 0.0
+            new_m = jnp.where(touched, beta_first * m + (1.0 - beta_first) * grad, m)
+            mean = jnp.mean(grad * grad, axis=1, keepdims=True)
+            new_v = jnp.where(touched, beta_second * v + (1.0 - beta_second) * mean, v)
+            scale = jnp.where(touched, 1.0 / (jnp.sqrt(new_v) + epsilon), 0.0)
+            new_s = new_m * scale
+            first = new_m if r == 0 else first + new_m
+            second = new_v if r == 0 else second + new_v
+            move = new_s if r == 0 else move + new_s
+        nm_ref[at, t, :] = first * (1.0 / reps)
+        nv_ref[t : t + 1, at] = flat(second, eye) * (1.0 / reps)
+        st_ref[at, t, :] = move * (1.0 / reps)
+
+
 def update_kernel(
     n, reps,
-    rows_ref, len_ref, w_ref, dense_ref, mark_ref, head_ref, emb_hbm, cross_hbm, hidden_hbm,
-    qi_ref, qo_ref, ga_ref,
-    emb, cross, hid, q_out, f_out, f_in, ct, before, g_out, locs,
-    load_sem, own_sem, qs, qr, rs, rr, gs, gr, xs, xr, fs, fr,
+    rows_ref, len_ref, w_ref, dense_ref, mark_ref, head_ref, v_ref,
+    emb_hbm, cross_hbm, hidden_hbm, m_hbm,
+    nm_ref, nv_ref, st_ref,
+    emb, cross, hid, mom, q_out, qi_ref, qo_ref, f_out, f_in, ct, before, g_out, ga_ref, locs,
+    sel, hit, acc,
+    load_sem, qs, qr, rs, rr, gs, gr, xs, xr, fs, fr,
 ):
     me = lax.axis_index("shard")
     rep = lax.axis_index("replica")
@@ -132,6 +170,8 @@
     load_emb.start()
     load_cross.start()
     load_hid.start()
+    load_mom = pltpu.make_async_copy(m_hbm, mom, load_sem.at[3])
+    load_mom.start()
 
     def exchange(src, dst, send, recv, t, d):
         to = lax.rem(me + d, n)
@@ -152,9 +192,7 @@
         lax.fori_loop(1, n, run, 0)
 
     def keep(src, dst, t):
-        copy = pltpu.make_async_copy(src.at[t, me], dst.at[t, me], own_sem)
-        copy.start()
-        copy.wait()
+        dst[t, me] = src[t, me]
 
     q_send = functools.partial(exchange, q_out, qi_ref, qs, qr)
     f_send = functools.partial(exchange, f_out, f_in, rs, rr)
@@ -196,9 +234,15 @@
         q_pass(r).start()
 
     for t in range(tables):
+        place_rows(qi_ref.at[t], sel.at[t, 0], hit.at[t, 0])
+    for t in range(tables):
         coefficients(
             n, own_rows, rows_ref[t], len_ref[t], w_ref[t], ranks[t], locs.at[t], ct.at[t]
         )
+    for r in range(1, reps):
+        q_pass(r).wait_recv()
+        for t in range(tables):
+            place_rows(qo_ref.at[r - 1, t], sel.at[t, r], hit.at[t, r])
     marks = column(mark_ref[...].astype(F32), diagonal(samples))
     heads = head_ref[...].astype(F32)
     lanes = heads.shape[1]
@@ -259,6 +303,7 @@
             device_id_type=MESH,
         )
 
+    load_mom.wait()
     for t in range(tables):
         for r in range(1, reps):
             pass_on(r, t, 0).start()
@@ -269,23 +314,33 @@
                 pass_on(r, t, d).start()
 
         each(relay)
+        acc[0] = dot(sel[t, 0], ga_ref[0, t].reshape(n * CAP, width), 1, 0)
+        for r in range(1, reps):
+            pass_on(r, t, 0).wait_recv()
+
+            def landed(d):
+                pass_on(r, t, d).wait_recv()
+
+            each(landed)
+            acc[r] = dot(sel[t, r], ga_ref[r, t].reshape(n * CAP, width), 1, 0)
+        adam_rows(reps, t, acc, hit, mom, v_ref, nm_ref, nv_ref, st_ref)
     for r in range(1, reps):
-        q_pass(r).wait()
+        q_pass(r).wait_send()
     for t in range(tables):
         for r in range(1, reps):
-            pass_on(r, t, 0).wait()
+            pass_on(r, t, 0).wait_send()
 
         def finish(d):
             q_send(t, d).wait_send()
             f_send(t, d).wait_send()
             g_send(t, d).wait_send()
             for r in range(1, reps):
-                pass_on(r, t, d).wait()
+                pass_on(r, t, d).wait_send()
 
         each(finish)
 
 
-def update(n, reps, rows, lengths, weights, dense, marks, head, embedding, cross, hidden):
+def update(n, reps, rows, lengths, weights, dense, marks, head, second, embedding, cross, hidden, first):
     tables, slots, samples = rows.shape
     own_rows, _, width = embedding.shape
     dma = pltpu.SemaphoreType.DMA
@@ -295,87 +350,62 @@
     return pl.pallas_call(
         functools.partial(update_kernel, n, reps),
         out_shape=(
-            jax.ShapeDtypeStruct((tables, n, 1, own_rows), F32),
-            jax.ShapeDtypeStruct((reps - 1, tables, n, 1, own_rows), F32),
-            jax.ShapeDtypeStruct((reps,) + blocks, BF16),
+            pltpu.VMEM(first.shape, F32),
+            pltpu.VMEM(second.shape, F32),
+            pltpu.VMEM(first.shape, F32),
         ),
-        in_specs=vmem(6) + [pl.BlockSpec(memory_space=pl.ANY)] * 3,
+        in_specs=vmem(7) + [pl.BlockSpec(memory_space=pl.ANY)] * 4,
         out_specs=tuple(vmem(3)),
         scratch_shapes=[
             pltpu.VMEM(embedding.shape, F32),
             pltpu.VMEM(cross.shape, BF16),
             pltpu.VMEM(hidden.shape, BF16),
+            pltpu.VMEM(first.shape, F32),
             pltpu.VMEM((tables, n, 1, own_rows), F32),
+            pltpu.VMEM((tables, n, 1, own_rows), F32),
+            pltpu.VMEM((reps - 1, tables, n, 1, own_rows), F32),
             pltpu.VMEM(blocks, BF16),
             pltpu.VMEM(blocks, BF16),
             pltpu.VMEM((tables, n * CAP, samples), BF16),
             pltpu.VMEM((samples, hidden.shape[1]), F32),
             pltpu.VMEM(blocks, BF16),
+            pltpu.VMEM((reps,) + blocks, BF16),
             pltpu.VMEM((tables, own_rows, slots * samples), BF16),
-            dma((3,)),
-            dma,
+            pltpu.VMEM((tables, reps, own_rows, n * CAP), BF16),
+            pltpu.VMEM((tables, reps, own_rows, 1), F32),
+            pltpu.VMEM((reps, own_rows, width), F32),
+            dma((4,)),
             pair, pair, pair, pair, pair, pair,
             dma((reps - 1,)), dma((reps - 1,)),
             wide, wide,
         ],
         compiler_params=pltpu.CompilerParams(collective_id=0, has_side_effects=True),
         name="update",
-    )(rows, lengths, weights, dense, marks, head, embedding, cross, hidden)
-
-
-def adam_kernel(reps, ga_ref, q_ref, qo_ref, m_ref, v_ref, nm_ref, nv_ref, st_ref):
-    tables, n, _, blk = q_ref.shape
-    width = m_ref.shape[2]
-    eye = diagonal(128)
-    for t in range(tables):
-        m = m_ref[:, t, :]
-        v = column(v_ref[t : t + 1, :], eye)
-        first = second = step = None
-        for r in range(reps):
-            src = q_ref if r == 0 else qo_ref.at[r - 1]
-            rows = [src[t, s] for s in range(n)]
-            named = rows[0]
-            for row in rows[1:]:
-                named = jnp.maximum(named, row)
-            touched = column(named, eye) >= 0.0
-            grad = dot(selector(rows), ga_ref[r, t].reshape(n * CAP, width), 0, 0)
-            new_m = jnp.where(touched, beta_first * m + (1.0 - beta_first) * grad, m)
-            mean = jnp.mean(grad * grad, axis=1, keepdims=True)
-            new_v = jnp.where(touched, beta_second * v + (1.0 - beta_second) * mean, v)
-            scale = jnp.where(touched, 1.0 / (jnp.sqrt(new_v) + epsilon), 0.0)
-            new_s = new_m * scale
-            first = new_m if r == 0 else first + new_m
-            second = new_v if r == 0 else second + new_v
-            step = new_s if r == 0 else step + new_s
-        nm_ref[:, t, :] = first * (1.0 / reps)
-        nv_ref[t : t + 1, :] = flat(second, eye) * (1.0 / reps)
-        st_ref[:, t, :] = step * (1.0 / reps)
-
-
-def adam(ga, q, qo, first_moment, second_moment, reps):
-    tables, n, _, own_rows = q.shape
-    width = first_moment.shape[2]
-    blk = own_rows // 2
-    mom = pl.BlockSpec((blk, tables, width), lambda i: (i, 0, 0))
-    sec = pl.BlockSpec((tables, blk), lambda i: (0, i))
+    )(rows, lengths, weights, dense, marks, head, second, embedding, cross, hidden, first)
+
+
+def emit_kernel(*refs):
+    count = (len(refs) - 1) // 2
+    sem = refs[-1]
+    copies = [
+        pltpu.make_async_copy(refs[i], refs[count + i], sem.at[i]) for i in range(count)
+    ]
+    for copy in copies:
+        copy.start()
+    for copy in copies:
+        copy.wait()
+
+
+def emit(*arrays):
+    count = len(arrays)
     return pl.pallas_call(
-        functools.partial(adam_kernel, reps),
-        out_shape=(
-            jax.ShapeDtypeStruct(first_moment.shape, F32),
-            jax.ShapeDtypeStruct(second_moment.shape, F32),
-            jax.ShapeDtypeStruct(first_moment.shape, F32),
-        ),
-        grid=(own_rows // blk,),
-        in_specs=[
-            pl.BlockSpec(ga.shape, lambda i: (0,) * 5, pipeline_mode=pl.Buffered(1)),
-            pl.BlockSpec((tables, n, 1, blk), lambda i: (0, 0, 0, i)),
-            pl.BlockSpec((reps - 1, tables, n, 1, blk), lambda i: (0, 0, 0, 0, i)),
-            mom,
-            sec,
-        ],
-        out_specs=(mom, sec, mom),
-        name="adam",
-    )(ga, q, qo, first_moment, second_moment)
+        emit_kernel,
+        out_shape=tuple(jax.ShapeDtypeStruct(a.shape, a.dtype) for a in arrays),
+        in_specs=vmem(count),
+        out_specs=tuple([pl.BlockSpec(memory_space=pl.ANY)] * count),
+        scratch_shapes=[pltpu.SemaphoreType.DMA((count,))],
+        name="emit",
+    )(*[pltpu.with_memory_space_constraint(a, pltpu.VMEM) for a in arrays])
 
 
 def local(
@@ -393,21 +423,22 @@
     hidden_weight,
     head_weight,
 ):
-    q, q_other, ga = update(
-        n,
-        reps,
-        jnp.transpose(bag_rows, (1, 2, 0)),
-        jnp.transpose(bag_lengths)[:, None, :],
-        jnp.transpose(bag_weights, (1, 2, 0)),
-        dense_input,
-        labels[None, :],
-        head_weight.reshape(-1, 128),
-        embedding,
-        cross_weight,
-        hidden_weight,
-    )
-    first, second, step = adam(
-        ga, q, q_other, first_moment, jnp.transpose(second_moment), reps
+    first, second, step = emit(
+        *update(
+            n,
+            reps,
+            jnp.transpose(bag_rows, (1, 2, 0)),
+            jnp.transpose(bag_lengths)[:, None, :],
+            jnp.transpose(bag_weights, (1, 2, 0)),
+            dense_input,
+            labels[None, :],
+            head_weight.reshape(-1, 128),
+            jnp.transpose(second_moment),
+            embedding,
+            cross_weight,
+            hidden_weight,
+            first_moment,
+        )
     )
     return first, jnp.transpose(second), step
 

time: 51 us -> 46.9 us (0.920)
  Pallas kernels: 50.1 us -> 46.1 us
    pallas_call x2, Pallas kernels: 50.1 us -> 46.1 us  [the longest x1 44.8 us: update(): pl.pallas_call(functools.partial(update_kernel, n, reps), out_shape=(pltp...]
where the time goes in v1:
time: 46.9 us; the launch traced here: 46.8 us
  Pallas kernels  46.1 us (98%)
  between operations  0.64 us (1%)
    pallas_call x1, Pallas kernels, update(): pl.pallas_call(functools.partial(update_kernel, n, reps), out_shape=(pltp...  44.8 us
    pallas_call x1, Pallas kernels, emit(): pl.pallas_call(emit_kernel, out_shape=tuple((jax.ShapeDtypeStruct(a.shape...  1.35 us

profile of v1, /device:TPU:1, one launch (start us, length us, event | category | flops | bytes accessed | tf_op | source)
XLA Modules:
  0.0 46.8 jit_solution(82806819218754136)
XLA Ops:
  0.6 44.8 %update.1 = (f32[512,2,256]{2,1,0:T(2,128)S(1)}, f32[2,512]{1,0:T(2,128)S(1)}, f32[512,2,256]{2,1,0:T(2,128)S(1)}) custom-call(s32[2,16,128]{2,1,0:T(8,128)} %bitcast.9, s32[2,1,128]{2,1,0:T(1,128)} %bitcast.13, bf16[2,16,128]{2,1,0:T(8,128)(2,1)} %bitcast.10, bf16[128,256]{1,0:T(8,128)(2,1)} %dense_ref.1, s32[1,128]{1,0:T(1,128)} %bitcast.14, ...), custom_call_target="tpu_custom_call" | custom-call | tf_op jit(solution)/shard_map/update/pallas_call | solution.py:350
  45.4 1.3 %emit.1 = (f32[512,2,256]{2,1,0:T(2,128)}, f32[2,512]{1,0:T(2,128)}, f32[512,2,256]{2,1,0:T(2,128)}) custom-call(f32[512,2,256]{2,1,0:T(2,128)S(1)} %get-tuple-element.9.refs_0_, f32[2,512]{1,0:T(2,128)S(1)} %get-tuple-element.10.refs_1_, f32[512,2,256]{2,1,0:T(2,128)S(1)} %get-tuple-element.11.refs_2_), custom_call_target="tpu_custom_call" | custom-call | tf_op jit(solution)/shard_map/emit/pallas_call | solution.py:401

commit v2 on v1

--- a/solution.py
+++ b/solution.py
@@ -23,6 +23,28 @@
 
 def vmem(count):
     return [pl.BlockSpec(memory_space=pltpu.VMEM)] * count
+
+
+LANES = 128
+
+
+def lane_rows(x):
+    rows, tables, width = x.shape
+    x = x.reshape(rows, tables, width // LANES, LANES)
+    return jnp.transpose(x, (0, 2, 1, 3)).reshape(-1, LANES)
+
+
+def table_rows(x, rows, tables):
+    x = jnp.transpose(x.reshape(rows, -1, tables, LANES), (0, 2, 1, 3))
+    return x.reshape(rows, tables, -1)
+
+
+def lane_slices(ref, tables, width, t, lo, count):
+    tiles = width // LANES
+    return [
+        pl.ds(lo * tiles * tables + i * tables + t, count, stride=tiles * tables)
+        for i in range(tiles)
+    ]
 
 
 def column(row, eye):
@@ -113,14 +135,16 @@
     hit_ref[...] = jnp.max(ranks, axis=1, keepdims=True)
 
 
-def adam_rows(reps, t, acc, hit, mom, v_ref, nm_ref, nv_ref, st_ref):
-    own_rows = v_ref.shape[1]
+def adam_rows(reps, t, acc, hit, mom, v_ref, vcol, nm_ref, nv_ref, st_ref):
+    tables, own_rows = v_ref.shape
+    width = acc.shape[2]
     step = 128
     eye = diagonal(step)
     for lo in range(0, own_rows, step):
         at = slice(lo, lo + step)
-        m = mom[at, t, :]
-        v = column(v_ref[t : t + 1, at], eye)
+        spots = lane_slices(mom, tables, width, t, lo, step)
+        m = jnp.concatenate([mom[spot, :] for spot in spots], axis=1)
+        v = vcol[t, at, :]
         first = second = move = None
         for r in range(reps):
             grad = acc[r, at, :]
@@ -133,9 +157,13 @@
             first = new_m if r == 0 else first + new_m
             second = new_v if r == 0 else second + new_v
             move = new_s if r == 0 else move + new_s
-        nm_ref[at, t, :] = first * (1.0 / reps)
+        first = first * (1.0 / reps)
+        move = move * (1.0 / reps)
+        for i, spot in enumerate(spots):
+            lanes = slice(i * LANES, (i + 1) * LANES)
+            nm_ref[spot, :] = first[:, lanes]
+            st_ref[spot, :] = move[:, lanes]
         nv_ref[t : t + 1, at] = flat(second, eye) * (1.0 / reps)
-        st_ref[at, t, :] = move * (1.0 / reps)
 
 
 def update_kernel(
@@ -144,13 +172,13 @@
     emb_hbm, cross_hbm, hidden_hbm, m_hbm,
     nm_ref, nv_ref, st_ref,
     emb, cross, hid, mom, q_out, qi_ref, qo_ref, f_out, f_in, ct, before, g_out, ga_ref, locs,
-    sel, hit, acc,
+    sel, hit, acc, vcol, lows,
     load_sem, qs, qr, rs, rr, gs, gr, xs, xr, fs, fr,
 ):
     me = lax.axis_index("shard")
     rep = lax.axis_index("replica")
     tables, slots, samples = rows_ref.shape
-    own_rows, _, width = emb.shape
+    own_rows, width = q_out.shape[3], f_out.shape[3]
     barrier = pltpu.get_barrier_semaphore()
 
     def hail(d, carry):
@@ -213,11 +241,28 @@
 
     load_emb.wait()
     for t in range(tables):
-        low = emb[:, t, :].astype(BF16)
-        each(lambda d: q_send(t, d).wait_recv())
-        got = dot(selector([qi_ref[t, s] for s in range(n)]), low, 1, 0).astype(BF16)
-        f_out[t] = got.reshape(n, CAP, width)
-        each(lambda d: f_send(t, d).start())
+        lows[t] = jnp.concatenate(
+            [emb[spot, :] for spot in lane_slices(emb, tables, width, t, 0, own_rows)], axis=1
+        ).astype(BF16)
+    group = 1 << (n.bit_length() // 2)
+    for base in range(n - group, -1, -group):
+        for t in range(tables):
+            for s in range(base, base + group):
+
+                @pl.when(me != s)
+                def _():
+                    q_send(t, lax.rem(me + n - s, n)).wait_recv()
+
+            picks = selector([qi_ref[t, s] for s in range(base, base + group)])
+            got = dot(picks, lows[t], 1, 0).astype(BF16)
+            f_out[t, base : base + group] = got.reshape(group, CAP, width)
+            for s in range(base, base + group):
+
+                @pl.when(me != s)
+                def _():
+                    f_send(t, lax.rem(s + n - me, n)).start()
+
+    for t in range(tables):
         keep(f_out, f_in, t)
 
     def q_pass(r):
@@ -235,6 +280,7 @@
 
     for t in range(tables):
         place_rows(qi_ref.at[t], sel.at[t, 0], hit.at[t, 0])
+        vcol[t] = column(v_ref[t : t + 1, :], diagonal(LANES))
     for t in range(tables):
         coefficients(
             n, own_rows, rows_ref[t], len_ref[t], w_ref[t], ranks[t], locs.at[t], ct.at[t]
@@ -323,7 +369,7 @@
 
             each(landed)
             acc[r] = dot(sel[t, r], ga_ref[r, t].reshape(n * CAP, width), 1, 0)
-        adam_rows(reps, t, acc, hit, mom, v_ref, nm_ref, nv_ref, st_ref)
+        adam_rows(reps, t, acc, hit, mom, v_ref, vcol, nm_ref, nv_ref, st_ref)
     for r in range(1, reps):
         q_pass(r).wait_send()
     for t in range(tables):
@@ -342,7 +388,8 @@
 
 def update(n, reps, rows, lengths, weights, dense, marks, head, second, embedding, cross, hidden, first):
     tables, slots, samples = rows.shape
-    own_rows, _, width = embedding.shape
+    own_rows = second.shape[1]
+    width = dense.shape[1]
     dma = pltpu.SemaphoreType.DMA
     blocks = (tables, n, CAP, width)
     pair = dma((tables, n))
@@ -374,6 +421,8 @@
             pltpu.VMEM((tables, reps, own_rows, n * CAP), BF16),
             pltpu.VMEM((tables, reps, own_rows, 1), F32),
             pltpu.VMEM((reps, own_rows, width), F32),
+            pltpu.VMEM((tables, own_rows, 1), F32),
+            pltpu.VMEM((tables, own_rows, width), BF16),
             dma((4,)),
             pair, pair, pair, pair, pair, pair,
             dma((reps - 1,)), dma((reps - 1,)),
@@ -434,13 +483,18 @@
             labels[None, :],
             head_weight.reshape(-1, 128),
             jnp.transpose(second_moment),
-            embedding,
+            lane_rows(embedding),
             cross_weight,
             hidden_weight,
-            first_moment,
-        )
-    )
-    return first, jnp.transpose(second), step
+            lane_rows(first_moment),
+        )
+    )
+    rows, tables, _ = embedding.shape
+    return (
+        table_rows(first, rows, tables),
+        jnp.transpose(second),
+        table_rows(step, rows, tables),
+    )
 
 
 def solution(mesh):

time: 46.9 us -> 45.4 us (0.968)
  Pallas kernels: 46.1 us -> 44.6 us
    pallas_call x1, Pallas kernels: 44.8 us -> 43.2 us  [update(): pl.pallas_call(functools.partial(update_kernel, n, reps), out_shape=(pltp...]
where the time goes in v2:
time: 45.4 us; the launch traced here: 45.2 us
  Pallas kernels  44.6 us (98%)
  between operations  0.64 us (1%)
    pallas_call x1, Pallas kernels, update(): pl.pallas_call(functools.partial(update_kernel, n, reps), out_shape=(pltp...  43.2 us
    pallas_call x1, Pallas kernels, emit(): pl.pallas_call(emit_kernel, out_shape=tuple((jax.ShapeDtypeStruct(a.shape...  1.35 us

profile of v2, /device:TPU:1, one launch (start us, length us, event | category | flops | bytes accessed | tf_op | source)
XLA Modules:
  0.0 45.2 jit_solution(3916851184149804583)
XLA Ops:
  0.6 43.2 %update.1 = (f32[2048,128]{1,0:T(8,128)S(1)}, f32[2,512]{1,0:T(2,128)S(1)}, f32[2048,128]{1,0:T(8,128)S(1)}) custom-call(s32[2,16,128]{2,1,0:T(8,128)} %bitcast.31, s32[2,1,128]{2,1,0:T(1,128)} %bitcast.35, bf16[2,16,128]{2,1,0:T(8,128)(2,1)} %bitcast.32, bf16[128,256]{1,0:T(8,128)(2,1)} %dense_ref.1, s32[1,128]{1,0:T(1,128)} %bitcast.36, ...), custom_call_target="tpu_custom_call" | custom-call | tf_op jit(solution)/shard_map/update/pallas_call | solution.py:397
  43.8 1.3 %emit.1 = (f32[2048,128]{1,0:T(8,128)}, f32[2,512]{1,0:T(2,128)}, f32[2048,128]{1,0:T(8,128)}) custom-call(f32[2048,128]{1,0:T(8,128)S(1)} %get-tuple-element.9.refs_0_, f32[2,512]{1,0:T(2,128)S(1)} %get-tuple-element.10.refs_1_, f32[2048,128]{1,0:T(8,128)S(1)} %get-tuple-element.11.refs_2_), custom_call_target="tpu_custom_call" | custom-call | tf_op jit(solution)/shard_map/emit/pallas_call | solution.py:450
